TPU v7x, 128 devices: a whole 4x4x4 slice. The times are simulated.
128 devices in a mesh: gx: 8 (over z, y_hi), gy: 16 (over x, y_lo, core).
Axes of the slice: x: 4, y: 4 (y_hi: 2, y_lo: 2; y = y_hi * 2 + y_lo), z: 4, core: 2. Of those that a mesh axis runs over, the one named last changes fastest.
Arguments:
- interior_inverse: bfloat16 [16, 16, 1536, 1536], P('gx', 'gy'), as said below
- coupling: bfloat16 [16, 16, 1536, 1024], P('gx', 'gy'), may hold values from -0.15625 to 0.15625
- face_stiffness: bfloat16 [16, 16, 4, 256, 256], P('gx', 'gy'), as said below
- corner_basis: bfloat16 [16, 16, 24, 1024], P('gx', 'gy'), may hold values from -0.25 to 0.25
- loads: float32 [16, 16, 4, 256], P('gx', 'gy'), may hold values from -48 to 48
- face_order: int32 [16, 16, 4, 256], P('gx', 'gy'), may hold values from 0 to 255, each once within a row
- corner_index: int32 [16, 16, 24], P('gx', 'gy'), may hold values from 0 to 1791, as said below
- coarse_inverse: float32 [1792, 1792], P(None, ('gx', 'gy')), as said below
Outputs:
- solution: float32 [16, 16, 4, 256], P('gx', 'gy')
- residual: float32 [16, 16, 4, 256], P('gx', 'gy')
Inputs may be any that keep to these rules, and one draw needn't show every extreme that they name: `interior_inverse`: symmetric positive definite. `face_stiffness`: each block is symmetric, and every subdomain's interface Schur complement is positive definite. `corner_index`: subdomains that share a grid vertex give its 6 coarse dofs the same indices in the same order (corners in the order top-left, top-right, bottom-left, bottom-right); the 24 indices of a subdomain are distinct; distinct vertices have distinct indices. `coarse_inverse`: symmetric positive definite.
All inputs are finite; a program needn't handle non-finite values.
Results may differ from a plain program's by a relative error of at most 0.01.
Values sent between devices are 32-bit elements; how exact they have to be, the bound alone decides.
No kernel may reach another device: no remote copies, remote signals or barrier semaphores. Data moves between devices by JAX's collectives and lax.ppermute only.
A program may use at most 128 MiB of HBM per device.

v0:
```python
import jax
import jax.numpy as jnp
from jax import lax
from jax.sharding import Mesh
from jax.sharding import PartitionSpec as P

ITERS = 2
GX = ("gx_0", "gx_1")
GY = ("gy_0", "gy_1", "gy_2")
GX_GY = ("gx_0", "gx_1", "gy_0", "gy_1", "gy_2")
careful = lax.Precision.HIGHEST


def from_behind(value, axis, steps):
    count = lax.axis_size(axis)
    first, last = (max(0, -steps), min(count, count - steps))
    return lax.ppermute(value, axis, [(source, source + steps) for source in range(first, last)])


def by_axis(array, axes):
    for axis in axes:
        array = lax.psum(array, axis)
    return array


def inverse_order(ordering):
    extent = ordering.shape[-1]
    levels = jnp.arange(extent, dtype=jnp.int32)
    matches = ordering[..., :, None] == levels
    return jnp.sum(jnp.where(matches, levels[:, None], 0), axis=-2)


def reorder(values, positions):
    return jnp.take_along_axis(values, positions, axis=-1)


def permute_block(matrix, ordering):
    extent = ordering.shape[-1]
    levels = jnp.arange(extent, dtype=jnp.int32)
    picker = (ordering[..., None, :] == levels[:, None]).astype(jnp.float32)
    rows_done = jnp.einsum("sfgk,sfkl->sfgl", picker, matrix, precision=careful)
    return jnp.einsum("sfgl,sfhl->sfgh", rows_done, picker, precision=careful)


def invert(summed):
    factor_low = jnp.linalg.cholesky(summed)
    identity = jnp.broadcast_to(jnp.eye(summed.shape[-1], dtype=jnp.float32), summed.shape)
    factor = lax.linalg.triangular_solve(factor_low, identity, left_side=True, lower=True)
    return jnp.einsum("...ik,...il->...kl", factor, factor, precision=careful)


def half_inner(first, second):
    return 0.5 * jnp.sum(first * second)


def swap_vectors(vector_in):
    from_above = from_behind(vector_in[-1, 1], GX, 1)
    from_below = from_behind(vector_in[0, 0], GX, -1)
    from_west = from_behind(vector_in[:, 3], GY, 1)
    from_east = from_behind(vector_in[:, 2], GY, -1)
    north_side = jnp.concatenate([from_above[None], vector_in[:-1, 1]], axis=0)
    south_side = jnp.concatenate([vector_in[1:, 0], from_below[None]], axis=0)
    return jnp.stack([north_side, south_side, from_west, from_east], axis=1)


def shards(
    interior_inverse,
    coupling,
    face_stiffness,
    corner_basis,
    loads,
    face_order,
    corner_index,
    coarse_inverse,
):
    local_count = interior_inverse.shape[0]
    inner_dofs = interior_inverse.shape[2]
    face_dofs = loads.shape[3]
    inverse_mat = interior_inverse.reshape(local_count, inner_dofs, inner_dofs)
    couple = coupling.reshape(local_count, inner_dofs, 4 * face_dofs)
    couple_faces = couple.reshape(local_count, inner_dofs, 4, face_dofs)
    stiffness = face_stiffness.reshape(local_count, 4, face_dofs, face_dofs)
    basis = corner_basis.reshape(local_count, corner_basis.shape[2], 4 * face_dofs)
    basis_wide = basis.astype(jnp.float32)
    ordering = face_order.reshape(local_count, 4, face_dofs)
    backward = inverse_order(ordering)
    corners = corner_index.reshape(local_count, corner_index.shape[2])
    coarse_total = coarse_inverse.shape[0]
    row_ids = lax.axis_index(GX) * local_count + jnp.arange(local_count, dtype=jnp.int32)
    col_id = lax.axis_index(GY)
    row_total = local_count * lax.axis_size(GX)
    col_total = lax.axis_size(GY)
    west_live = jnp.broadcast_to(col_id > 0, (local_count,))
    east_live = jnp.broadcast_to(col_id < col_total - 1, (local_count,))
    live_mask = jnp.stack(
        [row_ids > 0, row_ids < row_total - 1, west_live, east_live], axis=1
    ).astype(jnp.float32)[:, :, None]
    products = jnp.einsum(
        "sij,sjk->sik", inverse_mat, couple, preferred_element_type=jnp.float32
    ).astype(jnp.bfloat16)
    product_faces = products.reshape(local_count, inner_dofs, 4, face_dofs)
    schur_local = stiffness.astype(jnp.float32) - jnp.einsum(
        "sifk,sifl->sfkl", couple_faces, product_faces, preferred_element_type=jnp.float32
    )
    schur_canon = permute_block(schur_local, ordering)
    partner = from_behind(schur_canon[0, 0], GX, -1)
    partner_south = jnp.concatenate([schur_canon[1:, 0], partner[None]], axis=0)
    partner_side = from_behind(schur_canon[:, 2], GY, -1)
    south_inverse = invert(schur_canon[:, 1] + partner_south)
    east_inverse = invert(schur_canon[:, 3] + partner_side)
    top_inverse = from_behind(south_inverse[-1], GX, 1)
    north_inverse = jnp.concatenate([top_inverse[None], south_inverse[:-1]], axis=0)
    west_inverse = from_behind(east_inverse, GY, 1)
    face_inverse = jnp.stack([north_inverse, south_inverse, west_inverse, east_inverse], axis=1)
    loads_canon = reorder(loads.reshape(local_count, 4, face_dofs), backward)
    residual = live_mask * (loads_canon + swap_vectors(loads_canon))
    solution = jnp.zeros_like(residual)
    search = jnp.zeros_like(residual)
    along = jnp.zeros_like(residual)
    gamma_old = jnp.float32(1.0)
    alpha_old = jnp.float32(1.0)
    for iteration in range(ITERS):
        smoothed = jnp.einsum("sfkl,sfl->sfk", face_inverse, residual, precision=careful)
        share = jnp.einsum("sfkl,sfl->sfk", schur_canon, smoothed, precision=careful)
        share_local = (
            reorder(share, ordering).astype(jnp.bfloat16).reshape(local_count, 4 * face_dofs)
        )
        corner_res = jnp.einsum(
            "sjk,sk->sj", basis, share_local, preferred_element_type=jnp.float32
        )
        matches = (corners[:, :, None] == jnp.arange(coarse_total, dtype=jnp.int32)).astype(
            jnp.float32
        )
        dense = jnp.einsum("sj,sjg->g", corner_res, matches, precision=careful)
        owned = lax.psum_scatter(dense, GX_GY, scatter_dimension=0, tiled=True)
        partial_sol = jnp.dot(coarse_inverse, owned, precision=careful)
        coarse_sol = by_axis(partial_sol, GX_GY)
        corner_sol = jnp.einsum("sjg,g->sj", matches, coarse_sol, precision=careful)
        lifted = jnp.einsum("sjk,sj->sk", basis_wide, corner_sol, precision=careful).reshape(
            local_count, 4, face_dofs
        )
        spread = jnp.einsum(
            "sfkl,sfl->sfk", schur_canon, reorder(lifted, backward), precision=careful
        )
        precond_out = live_mask * jnp.einsum(
            "sfkl,sfl->sfk",
            face_inverse,
            residual + spread + swap_vectors(spread),
            precision=careful,
        )
        plain = reorder(precond_out, ordering).astype(jnp.bfloat16)
        middle = jnp.einsum(
            "sik,sk->si",
            couple,
            plain.reshape(local_count, 4 * face_dofs),
            preferred_element_type=jnp.float32,
        ).astype(jnp.bfloat16)
        solved = jnp.einsum(
            "sij,sj->si", inverse_mat, middle, preferred_element_type=jnp.float32
        ).astype(jnp.bfloat16)
        direct = jnp.einsum("sfkl,sfl->sfk", stiffness, plain, preferred_element_type=jnp.float32)
        back_part = jnp.einsum(
            "sifk,si->sfk", couple_faces, solved, preferred_element_type=jnp.float32
        )
        canon_out = reorder(direct - back_part, backward)
        image = live_mask * (canon_out + swap_vectors(canon_out))
        gamma, delta = (
            by_axis(half_inner(residual, precond_out), GX_GY),
            by_axis(half_inner(precond_out, image), GX_GY),
        )
        if iteration == 0:
            alpha = gamma / delta
            search = precond_out
            along = image
        else:
            beta = gamma / gamma_old
            alpha = gamma / (delta - beta * gamma / alpha_old)
            search = precond_out + beta * search
            along = image + beta * along
        solution = solution + alpha * search
        residual = residual - alpha * along
        gamma_old = gamma
        alpha_old = alpha
    return (
        solution.reshape(local_count, 1, 4, face_dofs),
        residual.reshape(local_count, 1, 4, face_dofs),
    )


def solution(mesh):
    torus = Mesh(mesh.devices.reshape(4, 2, 4, 2, 2), ("gx_0", "gx_1", "gy_0", "gy_1", "gy_2"))
    in_specs = (
        P(GX, GY, None, None),
        P(GX, GY, None, None),
        P(GX, GY, None, None, None),
        P(GX, GY, None, None),
        P(GX, GY, None, None),
        P(GX, GY, None, None),
        P(GX, GY, None),
        P(None, GX_GY),
    )
    out_specs = (P(GX, GY, None, None), P(GX, GY, None, None))
    return jax.shard_map(
        shards, mesh=torus, in_specs=in_specs, out_specs=out_specs, check_vma=False
    )
```

profile of v0, /device:TPU:1, one launch (start us, length us, event | category | flops | bytes accessed | tf_op | source)
XLA Modules:
  0.0 947.1 jit_solution(5315609379234085832)
XLA Ops:
  0.6 11.2 %reshape_reshape.3 = bf16[2,1536,4,256]{3,2,1,0:T(4,128)(2,1)} reshape(bf16[2,1,1536,1024]{3,2,1,0:T(8,128)(2,1)} %param.14) | data formatting | bytes 12582912 | tf_op jit(solution)/shard_map/reshape;reshape | solution.py:81
  11.9 16.5 %fusion.11 = bf16[2,1536,1024]{1,2,0:T(8,128)(2,1)} fusion(bf16[2,1,1536,1024]{3,2,1,0:T(8,128)(2,1)} %param.14, bf16[2,1,1536,1536]{3,2,1,0:T(8,128)(2,1)} %param.13), kind=kOutput, calls=%fused_computation.24 | convolution fusion | flops 9666822144 | bytes 22020096 | tf_op jit(solution)/shard_map/sij,sjk->sik/dot_general | solution.py:98
  48.4 20.4 %gather_fusion = f32[2048]{0:T(1024)S(1)} fusion(f32[2,4,256]{2,1,0:T(4,128)S(1)} %bitcast.383, s32[2048]{0:T(1024)S(1)} %bitcast.390), kind=kCustom, calls=%fused_computation.clone | custom fusion | bytes 40960 | tf_op jit(solution)/shard_map/jit(take_along_axis)/gather | solution.py:34
  103.6 23.5 %custom-call.36 = f32[2,128,128]{2,1,0:T(8,128)S(1)} custom-call(f32[2,128,128]{2,1,0:T(8,128)S(1)} %cholesky.198), custom_call_target="Cholesky" | custom-call | tf_op jit(solution)/shard_map/jit(cholesky)/cholesky | solution.py:46
  134.8 24.3 %custom-call.40 = f32[2,128,128]{2,1,0:T(8,128)S(1)} custom-call(f32[2,128,128]{2,1,0:T(8,128)} %cholesky.201), custom_call_target="Cholesky" | custom-call | tf_op jit(solution)/shard_map/jit(cholesky)/cholesky | solution.py:46
  160.5 21.1 %custom-call.37 = f32[2,1,128,128]{2,3,1,0:T(8,128)} custom-call(f32[2,1,128,128]{3,2,1,0:T(8,128)} %get-tuple-element.99), custom_call_target="InvertDiagBlocksLowerTriangular" | custom-call | tf_op jit(solution)/shard_map/jit(cholesky)/cholesky | solution.py:46
  185.4 25.0 %custom-call.38 = f32[2,128,128]{2,1,0:T(8,128)} custom-call(f32[2,128,128]{2,1,0:T(8,128)} %convolution_subtract_fusion.2), custom_call_target="Cholesky" | custom-call | tf_op jit(solution)/shard_map/jit(cholesky)/cholesky | solution.py:46
  210.5 21.1 %custom-call.41 = f32[2,1,128,128]{2,3,1,0:T(8,128)} custom-call(f32[2,1,128,128]{3,2,1,0:T(8,128)} %get-tuple-element.100), custom_call_target="InvertDiagBlocksLowerTriangular" | custom-call | tf_op jit(solution)/shard_map/jit(cholesky)/cholesky | solution.py:46
  236.2 24.9 %custom-call.42 = f32[2,128,128]{2,1,0:T(8,128)} custom-call(f32[2,128,128]{2,1,0:T(8,128)} %slice_subtract_fusion), custom_call_target="Cholesky" | custom-call | tf_op jit(solution)/shard_map/jit(cholesky)/cholesky | solution.py:46
  275.8 40.9 %custom-call.39 = f32[2,2,128,128]{2,3,1,0:T(8,128)} custom-call(f32[2,2,128,128]{3,2,1,0:T(8,128)} %bitcast.412), custom_call_target="InvertDiagBlocksLowerTriangular" | custom-call | tf_op jit(solution)/shard_map/triangular_solve/custom-call.0 | solution.py:48
  332.1 40.7 %custom-call.43 = f32[2,2,128,128]{2,3,1,0:T(8,128)} custom-call(f32[2,2,128,128]{3,2,1,0:T(8,128)} %bitcast.411), custom_call_target="InvertDiagBlocksLowerTriangular" | custom-call | tf_op jit(solution)/shard_map/triangular_solve/custom-call.0 | solution.py:48
  397.3 21.2 %gather_fusion.1 = bf16[2048]{0:T(1024)(128)(2,1)S(1)} fusion(bf16[2,4,256]{2,1,0:T(4,128)(2,1)S(1)} %bitcast.384, s32[2048]{0:T(1024)S(1)} %bitcast.386), kind=kCustom, calls=%fused_computation.1.clone | custom fusion | bytes 32768 | tf_op jit(solution)/shard_map/jit(take_along_axis)/gather | solution.py:34
  419.0 73.2 %all-reduce.1 = f32[1792]{0:T(1024)S(1)} all-reduce(f32[1792]{0:T(1024)S(1)} %convolution_reduce_fusion.3), channel_id=2, replica_groups=mesh['gx_0'=4,'gx_1'=2,'gy_0'=4,'gy_1'=2,'gy_2'=2] {'gx_0','gx_1','gy_0'..., use_global_device_ids=true, to_apply=%region_5.0.clone | all-reduce | flops 1792 | bytes 14336
  516.6 9.1 psum.214
  526.5 20.4 %gather_fusion.2 = f32[2048]{0:T(1024)S(1)} fusion(f32[2,4,256]{2,1,0:T(4,128)S(1)} %reshape.122, s32[2048]{0:T(1024)S(1)} %bitcast.393), kind=kCustom, calls=%fused_computation.2.clone | custom fusion | bytes 40960 | tf_op jit(solution)/shard_map/jit(take_along_axis)/gather | solution.py:34
  563.5 20.4 %gather_fusion.3 = bf16[2048]{0:T(1024)(128)(2,1)S(1)} fusion(f32[2,4,256]{2,1,0:T(4,128)S(1)} %bitcast_multiply_fusion.1, s32[2048]{0:T(1024)S(1)} %bitcast.387), kind=kCustom, calls=%fused_computation.3.clone | custom fusion | bytes 32768 | tf_op jit(solution)/shard_map/jit(take_along_axis)/gather | solution.py:34
  596.4 20.4 %gather_fusion.4 = f32[2048]{0:T(1024)S(1)} fusion(f32[2,4,256]{2,1,0:T(4,128)S(1)} %bitcast_subtract_fusion.3, s32[2048]{0:T(1024)S(1)} %bitcast.391), kind=kCustom, calls=%fused_computation.4.clone | custom fusion | bytes 40960 | tf_op jit(solution)/shard_map/jit(take_along_axis)/gather | solution.py:34
  633.4 10.4 %all-reduce.6 = (f32[]{:T(128)}, f32[]{:T(128)}) all-reduce(f32[]{:T(128)S(6)} %mul.109, f32[]{:T(128)S(6)} %mul.112), channel_id=1, replica_groups=mesh['gx_0'=4,'gx_1'=2,'gy_0'=4,'gy_1'=2,'gy_2'=2] {'gx_0'}, use_global_device_ids=true, to_apply=%region_12.0 | all-reduce | flops 2 | bytes 16 | tf_op jit(solution)/shard_map/psum | solution.py:22
  678.2 20.8 %gather_fusion.5 = bf16[2048]{0:T(1024)(128)(2,1)S(1)} fusion(bf16[2,4,256]{2,1,0:T(4,128)(2,1)S(1)} %bitcast.385, s32[2048]{0:T(1024)S(1)} %bitcast.388), kind=kCustom, calls=%fused_computation.5.clone | custom fusion | bytes 32768 | tf_op jit(solution)/shard_map/jit(take_along_axis)/gather | solution.py:34
  699.5 61.9 %all-reduce.2 = f32[1792]{0:T(1024)S(1)} all-reduce(f32[1792]{0:T(1024)S(1)} %convolution_reduce_fusion.2), channel_id=3, replica_groups=mesh['gx_0'=4,'gx_1'=2,'gy_0'=4,'gy_1'=2,'gy_2'=2] {'gx_0','gx_1','gy_0'..., use_global_device_ids=true, to_apply=%region_23.0.clone | all-reduce | flops 1792 | bytes 14336
  795.7 20.4 %gather_fusion.6 = f32[2048]{0:T(1024)S(1)} fusion(f32[2,4,256]{2,1,0:T(4,128)S(1)} %reshape.125, s32[2048]{0:T(1024)S(1)} %bitcast.394), kind=kCustom, calls=%fused_computation.6.clone | custom fusion | bytes 40960 | tf_op jit(solution)/shard_map/jit(take_along_axis)/gather | solution.py:34
  832.1 20.4 %gather_fusion.7 = bf16[2048]{0:T(1024)(128)(2,1)S(1)} fusion(f32[2,4,256]{2,1,0:T(4,128)S(1)} %bitcast_multiply_fusion, s32[2048]{0:T(1024)S(1)} %bitcast.389), kind=kCustom, calls=%fused_computation.7.clone | custom fusion | bytes 32768 | tf_op jit(solution)/shard_map/jit(take_along_axis)/gather | solution.py:34
  864.9 20.4 %gather_fusion.8 = f32[2048]{0:T(1024)S(1)} fusion(f32[2,4,256]{2,1,0:T(4,128)S(1)} %bitcast_subtract_fusion.2, s32[2048]{0:T(1024)S(1)} %bitcast.392), kind=kCustom, calls=%fused_computation.8.clone | custom fusion | bytes 40960 | tf_op jit(solution)/shard_map/jit(take_along_axis)/gather | solution.py:34
  902.1 10.9 %all-reduce.5 = (f32[]{:T(128)}, f32[]{:T(128)}) all-reduce(f32[]{:T(128)S(6)} %mul.118, f32[]{:T(128)S(6)} %mul.121), channel_id=1, replica_groups=mesh['gx_0'=4,'gx_1'=2,'gy_0'=4,'gy_1'=2,'gy_2'=2] {'gx_0'}, use_global_device_ids=true, to_apply=%region_30.0 | all-reduce | flops 2 | bytes 16 | tf_op jit(solution)/shard_map/psum | solution.py:22
  (332 shorter events, 354.3 us)
Async XLA Ops:
  39.9 57.4 %collective-permute-start.4 = (f32[256,256]{0,1:T(8,128)}, f32[256,256]{0,1:T(8,128)}, u32[]{:S(2)}, u32[]{:S(2)}) collective-permute-start(f32[256,256]{0,1:T(8,128)} %bitcast.410), channel_id=1, source_target_pairs={{16,0},{32,16},{48,32},{64,48},{80,64},{96,80},{112,96},{17,1},{33... | collective-permute-start | bytes 786440 | tf_op jit(solution)/shard_map/ppermute | solution.py:17
  44.6 83.3 %collective-permute-start.6 = (f32[2,256,256]{1,2,0:T(8,128)}, f32[2,256,256]{1,2,0:T(8,128)}, u32[]{:S(2)}, u32[]{:S(2)}) collective-permute-start(f32[2,256,256]{1,2,0:T(8,128)} %bitcast.409), channel_id=1, source_target_pairs={{1,0},{2,1},{3,2},{4,3},{5,4},{6,5},{7,6},{8,7},{9,8},{10,9},{11,1... | collective-permute-start | bytes 1572872 | tf_op jit(solution)/shard_map/ppermute | solution.py:17
  70.1 24.0 %collective-permute-start = (f32[256]{0:T(256)}, f32[256]{0:T(256)}, u32[]{:S(2)}, u32[]{:S(2)}) collective-permute-start(f32[256]{0:T(256)} %bitcast.3), channel_id=1, source_target_pairs={{0,16},{16,32},{32,48},{48,64},{64,80},{80,96},{96,112},{1,17},{17... | collective-permute-start | bytes 3080 | tf_op jit(solution)/shard_map/ppermute | solution.py:17
  76.3 311.7 %collective-permute-start.1 = (f32[256]{0:T(256)}, f32[256]{0:T(256)}, u32[]{:S(2)}, u32[]{:S(2)}) collective-permute-start(f32[256]{0:T(256)} %bitcast.7), channel_id=1, source_target_pairs={{16,0},{32,16},{48,32},{64,48},{80,64},{96,80},{112,96},{17,1},{33... | collective-permute-start | bytes 3080 | tf_op jit(solution)/shard_map/ppermute | solution.py:17
  78.2 310.5 %collective-permute-start.2 = (f32[2,256]{1,0:T(2,128)}, f32[2,256]{1,0:T(2,128)}, u32[]{:S(2)}, u32[]{:S(2)}) collective-permute-start(f32[2,256]{1,0:T(2,128)} %get-tuple-element.129), channel_id=1, source_target_pairs={{0,1},{1,2},{2,3},{3,4},{4,5},{5,6},{6,7},{7,8},{8,9},{9,10},{10,1... | collective-permute-start | bytes 6152 | tf_op jit(solution)/shard_map/ppermute | solution.py:17
  94.1 295.3 %collective-permute-start.3 = (f32[2,256]{1,0:T(2,128)}, f32[2,256]{1,0:T(2,128)}, u32[]{:S(2)}, u32[]{:S(2)}) collective-permute-start(f32[2,256]{1,0:T(2,128)} %get-tuple-element.130), channel_id=1, source_target_pairs={{1,0},{2,1},{3,2},{4,3},{5,4},{6,5},{7,6},{8,7},{9,8},{10,9},{11,1... | collective-permute-start | bytes 6152 | tf_op jit(solution)/shard_map/ppermute | solution.py:17
  378.0 15.5 %collective-permute-start.7 = (f32[2,256,256]{2,1,0:T(8,128)S(1)}, f32[2,256,256]{2,1,0:T(8,128)S(1)}, u32[]{:S(2)}, u32[]{:S(2)}) collective-permute-start(f32[2,256,256]{2,1,0:T(8,128)S(1)} %fusion.44), channel_id=1, source_target_pairs={{0,1},{1,2},{2,3},{3,4},{4,5},{5,6},{6,7},{7,8},{8,9},{9,10},{10,1... | collective-permute-start | bytes 1572872 | tf_op jit(solution)/shard_map/ppermute | solution.py:17
  381.7 11.8 %collective-permute-start.5 = (f32[256,256]{1,0:T(8,128)S(1)}, f32[256,256]{1,0:T(8,128)S(1)}, u32[]{:S(2)}, u32[]{:S(2)}) collective-permute-start(f32[256,256]{1,0:T(8,128)S(1)} %get-tuple-element.91), channel_id=1, source_target_pairs={{0,16},{16,32},{32,48},{48,64},{64,80},{80,96},{96,112},{1,17},{17... | collective-permute-start | bytes 786440 | tf_op jit(solution)/shard_map/ppermute | solution.py:17
  548.9 9.6 %collective-permute-start.8 = (f32[256]{0:T(256)S(1)}, f32[256]{0:T(256)S(1)}, u32[]{:S(2)}, u32[]{:S(2)}) collective-permute-start(f32[256]{0:T(256)S(1)} %bitcast.451), channel_id=1, source_target_pairs={{0,16},{16,32},{32,48},{48,64},{64,80},{80,96},{96,112},{1,17},{17... | collective-permute-start | bytes 3080 | tf_op jit(solution)/shard_map/ppermute | solution.py:17
  551.7 6.8 collective-permute-start.9
  553.0 5.6 collective-permute-start.10
  556.6 4.9 collective-permute-start.11
  616.8 12.0 %collective-permute-start.12 = (f32[256]{0:T(256)S(1)}, f32[256]{0:T(256)S(1)}, u32[]{:S(2)}, u32[]{:S(2)}) collective-permute-start(f32[256]{0:T(256)S(1)} %bitcast.452), channel_id=1, source_target_pairs={{0,16},{16,32},{32,48},{48,64},{64,80},{80,96},{96,112},{1,17},{17... | collective-permute-start | bytes 3080 | tf_op jit(solution)/shard_map/ppermute | solution.py:17
  623.2 5.8 collective-permute-start.13
  624.5 4.5 collective-permute-start.14
  626.5 4.9 collective-permute-start.15
  818.1 9.3 collective-permute-start.16
  820.6 6.8 collective-permute-start.17
  821.9 5.6 collective-permute-start.18
  825.2 4.9 collective-permute-start.19
  885.4 12.0 %collective-permute-start.20 = (f32[256]{0:T(256)S(1)}, f32[256]{0:T(256)S(1)}, u32[]{:S(2)}, u32[]{:S(2)}) collective-permute-start(f32[256]{0:T(256)S(1)} %bitcast.454), channel_id=1, source_target_pairs={{0,16},{16,32},{32,48},{48,64},{64,80},{80,96},{96,112},{1,17},{17... | collective-permute-start | bytes 3080 | tf_op jit(solution)/shard_map/ppermute | solution.py:17
  891.8 5.8 collective-permute-start.21
  893.1 4.5 collective-permute-start.22
  895.1 5.0 collective-permute-start.23
  (36 other events, 1014.8 us)
where the time goes:
time: 958 us; the launch traced here: 947 us
  blocking collectives  278 us (29%)
  other arithmetic  246 us (26%)
  local copies, waits for them, and re-layouts  239 us (25%)
  matrix products  88.5 us (9%)
  starting transfers between devices  70.9 us (7%)
  waiting for transfers between devices  13.9 us (1%)
  between operations  10.7 us (1%)
    gather x19, local copies, waits for them, and re-layouts, reorder(): return jnp.take_along_axis(values, positions, axis=-1)  185 us
    another operation x14, other arithmetic, invert(): factor_low = jnp.linalg.cholesky(summed)  145 us
    psum x20, blocking collectives, by_axis(): array = lax.psum(array, axis)  143 us
    unnamed x2, blocking collectives  135 us
    another operation x5, other arithmetic, invert(): lax.linalg.triangular_solve(factor_low, identity, left_side=True, lower=T...  85.3 us
    ppermute x24, starting transfers between devices, from_behind(): lax.ppermute(value, axis, [(source, source + steps) for source in range(f...  70.9 us
    another operation x16, local copies, waits for them, and re-layouts, invert(): lax.linalg.triangular_solve(factor_low, identity, left_side=True, lower=T...  20.3 us
  transfers between devices with their start and end apart: 24, of which 7 were waited for; matrix products, arithmetic and copies ran while one was open for 34% of the time, Pallas kernels for 0%

commit v1 on v0

--- a/solution.py
+++ b/solution.py
@@ -19,7 +19,11 @@
 
 def by_axis(array, axes):
     for axis in axes:
-        array = lax.psum(array, axis)
+
+        def _track_series(message):
+            return jnp.sum(lax.all_gather(message, axis_name=axis), axis=0)
+
+        array = _track_series(array)
     return array
 
 

time: 958 us -> 1000 us (1.044)
  local copies, waits for them, and re-layouts: 239 us -> 267 us
  other arithmetic: 246 us -> 258 us
    psum x20 -> x0, blocking collectives: 143 us -> none  [by_axis(): array = lax.psum(array, axis)]
    unnamed x2 -> x12, blocking collectives: 135 us -> 209 us
    all_gather x0 -> x10, blocking collectives: none -> 72.6 us  [_track_series(): return jnp.sum(lax.all_gather(message, axis_name=axis), axis=0)]
    unnamed x81 -> x142, local copies, waits for them, and re-layouts: 11.2 us -> 39.5 us
    reduce_sum x0 -> x30, other arithmetic: none -> 12.5 us  [_track_series(): return jnp.sum(lax.all_gather(message, axis_name=axis), axis=0)]
  transfers between devices with their start and end apart: 24 -> 24, of which waited for: 7 -> 7; matrix products, arithmetic and copies ran while one was open for 34% -> 32% of each run, Pallas kernels for 0% -> 0%
where the time goes in v1:
time: 1000 us; the launch traced here: 992 us
  blocking collectives  282 us (28%)
  local copies, waits for them, and re-layouts  267 us (27%)
  other arithmetic  258 us (26%)
  matrix products  88.4 us (9%)
  starting transfers between devices  72 us (7%)
  waiting for transfers between devices  13.7 us (1%)
  between operations  10.9 us (1%)
    unnamed x12, blocking collectives  209 us
    gather x19, local copies, waits for them, and re-layouts, reorder(): return jnp.take_along_axis(values, positions, axis=-1)  185 us
    another operation x14, other arithmetic, invert(): factor_low = jnp.linalg.cholesky(summed)  145 us
    another operation x5, other arithmetic, invert(): lax.linalg.triangular_solve(factor_low, identity, left_side=True, lower=T...  85.3 us
    all_gather x10, blocking collectives, _track_series(): return jnp.sum(lax.all_gather(message, axis_name=axis), axis=0)  72.6 us
    ppermute x24, starting transfers between devices, from_behind(): lax.ppermute(value, axis, [(source, source + steps) for source in range(f...  72 us
    unnamed x142, local copies, waits for them, and re-layouts  39.5 us
  transfers between devices with their start and end apart: 24, of which 7 were waited for; matrix products, arithmetic and copies ran while one was open for 32% of the time, Pallas kernels for 0%

profile of v1, /device:TPU:1, one launch (start us, length us, event | category | flops | bytes accessed | tf_op | source)
XLA Modules:
  0.0 992.3 jit_solution(9871750573484048726)
XLA Ops:
  0.6 11.2 %reshape_reshape.3 = bf16[2,1536,4,256]{3,2,1,0:T(4,128)(2,1)} reshape(bf16[2,1,1536,1024]{3,2,1,0:T(8,128)(2,1)} %param.14) | data formatting | bytes 12582912 | tf_op jit(solution)/shard_map/reshape;reshape | solution.py:85
  11.9 16.5 %fusion.11 = bf16[2,1536,1024]{1,2,0:T(8,128)(2,1)} fusion(bf16[2,1,1536,1024]{3,2,1,0:T(8,128)(2,1)} %param.14, bf16[2,1,1536,1536]{3,2,1,0:T(8,128)(2,1)} %param.13), kind=kOutput, calls=%fused_computation.24 | convolution fusion | flops 9666822144 | bytes 22020096 | tf_op jit(solution)/shard_map/sij,sjk->sik/dot_general | solution.py:102
  48.4 20.4 %gather_fusion = f32[2048]{0:T(1024)S(1)} fusion(f32[2,4,256]{2,1,0:T(4,128)S(1)} %bitcast.412, s32[2048]{0:T(1024)S(1)} %bitcast.419), kind=kCustom, calls=%fused_computation.clone | custom fusion | bytes 40960 | tf_op jit(solution)/shard_map/jit(take_along_axis)/gather | solution.py:38
  104.8 23.5 %custom-call.36 = f32[2,128,128]{2,1,0:T(8,128)S(1)} custom-call(f32[2,128,128]{2,1,0:T(8,128)S(1)} %cholesky.198), custom_call_target="Cholesky" | custom-call | tf_op jit(solution)/shard_map/jit(cholesky)/cholesky | solution.py:50
  136.1 24.3 %custom-call.40 = f32[2,128,128]{2,1,0:T(8,128)S(1)} custom-call(f32[2,128,128]{2,1,0:T(8,128)} %cholesky.201), custom_call_target="Cholesky" | custom-call | tf_op jit(solution)/shard_map/jit(cholesky)/cholesky | solution.py:50
  161.8 21.1 %custom-call.37 = f32[2,1,128,128]{2,3,1,0:T(8,128)} custom-call(f32[2,1,128,128]{3,2,1,0:T(8,128)} %get-tuple-element.99), custom_call_target="InvertDiagBlocksLowerTriangular" | custom-call | tf_op jit(solution)/shard_map/jit(cholesky)/cholesky | solution.py:50
  186.7 25.0 %custom-call.38 = f32[2,128,128]{2,1,0:T(8,128)} custom-call(f32[2,128,128]{2,1,0:T(8,128)} %convolution_subtract_fusion.2), custom_call_target="Cholesky" | custom-call | tf_op jit(solution)/shard_map/jit(cholesky)/cholesky | solution.py:50
  211.8 21.1 %custom-call.41 = f32[2,1,128,128]{2,3,1,0:T(8,128)} custom-call(f32[2,1,128,128]{3,2,1,0:T(8,128)} %get-tuple-element.100), custom_call_target="InvertDiagBlocksLowerTriangular" | custom-call | tf_op jit(solution)/shard_map/jit(cholesky)/cholesky | solution.py:50
  237.5 24.9 %custom-call.42 = f32[2,128,128]{2,1,0:T(8,128)} custom-call(f32[2,128,128]{2,1,0:T(8,128)} %slice_subtract_fusion), custom_call_target="Cholesky" | custom-call | tf_op jit(solution)/shard_map/jit(cholesky)/cholesky | solution.py:50
  276.9 40.9 %custom-call.39 = f32[2,2,128,128]{2,3,1,0:T(8,128)} custom-call(f32[2,2,128,128]{3,2,1,0:T(8,128)} %bitcast.440), custom_call_target="InvertDiagBlocksLowerTriangular" | custom-call | tf_op jit(solution)/shard_map/triangular_solve/custom-call.0 | solution.py:52
  333.0 40.7 %custom-call.43 = f32[2,2,128,128]{2,3,1,0:T(8,128)} custom-call(f32[2,2,128,128]{3,2,1,0:T(8,128)} %bitcast.441), custom_call_target="InvertDiagBlocksLowerTriangular" | custom-call | tf_op jit(solution)/shard_map/triangular_solve/custom-call.0 | solution.py:52
  398.2 21.2 %gather_fusion.1 = bf16[2048]{0:T(1024)(128)(2,1)S(1)} fusion(bf16[2,4,256]{2,1,0:T(4,128)(2,1)S(1)} %bitcast.413, s32[2048]{0:T(1024)S(1)} %bitcast.415), kind=kCustom, calls=%fused_computation.1.clone | custom fusion | bytes 32768 | tf_op jit(solution)/shard_map/jit(take_along_axis)/gather | solution.py:38
  419.9 73.3 %all-reduce.21 = f32[1792]{0:T(1024)S(1)} all-reduce(f32[1792]{0:T(1024)S(1)} %convolution_reduce_fusion.1), channel_id=12, replica_groups=mesh['gx_0'=4,'gx_1'=2,'gy_0'=4,'gy_1'=2,'gy_2'=2] {'gx_0','gx_1','gy_0'..., use_global_device_ids=true, to_apply=%region_5.0.clone | all-reduce | flops 1792 | bytes 14336
  530.8 20.4 %gather_fusion.2 = f32[2048]{0:T(1024)S(1)} fusion(f32[2,4,256]{2,1,0:T(4,128)S(1)} %reshape.122, s32[2048]{0:T(1024)S(1)} %bitcast.422), kind=kCustom, calls=%fused_computation.2.clone | custom fusion | bytes 40960 | tf_op jit(solution)/shard_map/jit(take_along_axis)/gather | solution.py:38
  567.8 20.4 %gather_fusion.3 = bf16[2048]{0:T(1024)(128)(2,1)S(1)} fusion(f32[2,4,256]{2,1,0:T(4,128)S(1)} %bitcast_multiply_fusion.1, s32[2048]{0:T(1024)S(1)} %bitcast.416), kind=kCustom, calls=%fused_computation.3.clone | custom fusion | bytes 32768 | tf_op jit(solution)/shard_map/jit(take_along_axis)/gather | solution.py:38
  600.7 20.4 %gather_fusion.4 = f32[2048]{0:T(1024)S(1)} fusion(f32[2,4,256]{2,1,0:T(4,128)S(1)} %bitcast_subtract_fusion.3, s32[2048]{0:T(1024)S(1)} %bitcast.420), kind=kCustom, calls=%fused_computation.4.clone | custom fusion | bytes 40960 | tf_op jit(solution)/shard_map/jit(take_along_axis)/gather | solution.py:38
  639.9 10.9 %all-reduce.26 = (f32[4]{0:T(128)S(1)}, f32[4]{0:T(128)S(1)}) all-reduce(f32[4]{0:T(128)S(1)} %dynamic-update-slice.9, f32[4]{0:T(128)S(1)} %dynamic-update-slice.14), channel_id=1, replica_groups=mesh['gx_0'=4,'gx_1'=2,'gy_0'=4,'gy_1'=2,'gy_2'=2] {'gx_0'}, use_global_device_ids=true, to_apply=%add.1 | all-reduce | flops 8 | bytes 64
  702.5 20.8 %gather_fusion.5 = bf16[2048]{0:T(1024)(128)(2,1)S(1)} fusion(bf16[2,4,256]{2,1,0:T(4,128)(2,1)S(1)} %bitcast.414, s32[2048]{0:T(1024)S(1)} %bitcast.417), kind=kCustom, calls=%fused_computation.5.clone | custom fusion | bytes 32768 | tf_op jit(solution)/shard_map/jit(take_along_axis)/gather | solution.py:38
  723.7 61.9 %all-reduce.22 = f32[1792]{0:T(1024)S(1)} all-reduce(f32[1792]{0:T(1024)S(1)} %convolution_reduce_fusion), channel_id=13, replica_groups=mesh['gx_0'=4,'gx_1'=2,'gy_0'=4,'gy_1'=2,'gy_2'=2] {'gx_0','gx_1','gy_0'..., use_global_device_ids=true, to_apply=%region_23.0.clone | all-reduce | flops 1792 | bytes 14336
  812.3 10.1 %all-gather.19 = f32[2,1,1792]{2,1,0:T(1,128)S(1)} all-gather(f32[1,1,1792]{2,1,0:T(1,128)S(1)} %reshape.350), channel_id=11, replica_groups=mesh['gx_0'=4,'gx_1'=2,'gy_0'=4,'gy_1'=2,'gy_2'=2] {'gy_2'}, dimensions={0}, use_global_device_ids=true | all-gather | bytes 21504 | tf_op jit(solution)/shard_map/all_gather | solution.py:24
  823.3 20.4 %gather_fusion.6 = f32[2048]{0:T(1024)S(1)} fusion(f32[2,4,256]{2,1,0:T(4,128)S(1)} %reshape.125, s32[2048]{0:T(1024)S(1)} %bitcast.423), kind=kCustom, calls=%fused_computation.6.clone | custom fusion | bytes 40960 | tf_op jit(solution)/shard_map/jit(take_along_axis)/gather | solution.py:38
  860.8 20.4 %gather_fusion.7 = bf16[2048]{0:T(1024)(128)(2,1)S(1)} fusion(f32[2,4,256]{2,1,0:T(4,128)S(1)} %bitcast_multiply_fusion, s32[2048]{0:T(1024)S(1)} %bitcast.418), kind=kCustom, calls=%fused_computation.7.clone | custom fusion | bytes 32768 | tf_op jit(solution)/shard_map/jit(take_along_axis)/gather | solution.py:38
  893.7 20.4 %gather_fusion.8 = f32[2048]{0:T(1024)S(1)} fusion(f32[2,4,256]{2,1,0:T(4,128)S(1)} %bitcast_subtract_fusion.2, s32[2048]{0:T(1024)S(1)} %bitcast.421), kind=kCustom, calls=%fused_computation.8.clone | custom fusion | bytes 40960 | tf_op jit(solution)/shard_map/jit(take_along_axis)/gather | solution.py:38
  932.1 10.5 %all-reduce.25 = (f32[4]{0:T(128)S(1)}, f32[4]{0:T(128)S(1)}) all-reduce(f32[4]{0:T(128)S(1)} %dynamic-update-slice.19, f32[4]{0:T(128)S(1)} %dynamic-update-slice.24), channel_id=1, replica_groups=mesh['gx_0'=4,'gx_1'=2,'gy_0'=4,'gy_1'=2,'gy_2'=2] {'gx_0'}, use_global_device_ids=true, to_apply=%add.11 | all-reduce | flops 8 | bytes 64
  (423 shorter events, 397.9 us)
Async XLA Ops:
  39.9 58.6 %collective-permute-start.4 = (f32[256,256]{0,1:T(8,128)}, f32[256,256]{0,1:T(8,128)}, u32[]{:S(2)}, u32[]{:S(2)}) collective-permute-start(f32[256,256]{0,1:T(8,128)} %bitcast.439), channel_id=1, source_target_pairs={{16,0},{32,16},{48,32},{64,48},{80,64},{96,80},{112,96},{17,1},{33... | collective-permute-start | bytes 786440 | tf_op jit(solution)/shard_map/ppermute | solution.py:17
  44.6 84.6 %collective-permute-start.6 = (f32[2,256,256]{1,2,0:T(8,128)}, f32[2,256,256]{1,2,0:T(8,128)}, u32[]{:S(2)}, u32[]{:S(2)}) collective-permute-start(f32[2,256,256]{1,2,0:T(8,128)} %bitcast.438), channel_id=1, source_target_pairs={{1,0},{2,1},{3,2},{4,3},{5,4},{6,5},{7,6},{8,7},{9,8},{10,9},{11,1... | collective-permute-start | bytes 1572872 | tf_op jit(solution)/shard_map/ppermute | solution.py:17
  70.1 25.2 %collective-permute-start = (f32[256]{0:T(256)}, f32[256]{0:T(256)}, u32[]{:S(2)}, u32[]{:S(2)}) collective-permute-start(f32[256]{0:T(256)} %bitcast.3), channel_id=1, source_target_pairs={{0,16},{16,32},{32,48},{48,64},{64,80},{80,96},{96,112},{1,17},{17... | collective-permute-start | bytes 3080 | tf_op jit(solution)/shard_map/ppermute | solution.py:17
  76.4 312.6 %collective-permute-start.1 = (f32[256]{0:T(256)}, f32[256]{0:T(256)}, u32[]{:S(2)}, u32[]{:S(2)}) collective-permute-start(f32[256]{0:T(256)} %bitcast.7), channel_id=1, source_target_pairs={{16,0},{32,16},{48,32},{64,48},{80,64},{96,80},{112,96},{17,1},{33... | collective-permute-start | bytes 3080 | tf_op jit(solution)/shard_map/ppermute | solution.py:17
  78.3 311.4 %collective-permute-start.2 = (f32[2,256]{1,0:T(2,128)}, f32[2,256]{1,0:T(2,128)}, u32[]{:S(2)}, u32[]{:S(2)}) collective-permute-start(f32[2,256]{1,0:T(2,128)} %get-tuple-element.129), channel_id=1, source_target_pairs={{0,1},{1,2},{2,3},{3,4},{4,5},{5,6},{6,7},{7,8},{8,9},{9,10},{10,1... | collective-permute-start | bytes 6152 | tf_op jit(solution)/shard_map/ppermute | solution.py:17
  95.3 295.0 %collective-permute-start.3 = (f32[2,256]{1,0:T(2,128)}, f32[2,256]{1,0:T(2,128)}, u32[]{:S(2)}, u32[]{:S(2)}) collective-permute-start(f32[2,256]{1,0:T(2,128)} %get-tuple-element.130), channel_id=1, source_target_pairs={{1,0},{2,1},{3,2},{4,3},{5,4},{6,5},{7,6},{8,7},{9,8},{10,9},{11,1... | collective-permute-start | bytes 6152 | tf_op jit(solution)/shard_map/ppermute | solution.py:17
  378.8 15.5 %collective-permute-start.7 = (f32[2,256,256]{2,1,0:T(8,128)S(1)}, f32[2,256,256]{2,1,0:T(8,128)S(1)}, u32[]{:S(2)}, u32[]{:S(2)}) collective-permute-start(f32[2,256,256]{2,1,0:T(8,128)S(1)} %fusion.44), channel_id=1, source_target_pairs={{0,1},{1,2},{2,3},{3,4},{4,5},{5,6},{6,7},{7,8},{8,9},{9,10},{10,1... | collective-permute-start | bytes 1572872 | tf_op jit(solution)/shard_map/ppermute | solution.py:17
  382.6 11.7 %collective-permute-start.5 = (f32[256,256]{1,0:T(8,128)S(1)}, f32[256,256]{1,0:T(8,128)S(1)}, u32[]{:S(2)}, u32[]{:S(2)}) collective-permute-start(f32[256,256]{1,0:T(8,128)S(1)} %get-tuple-element.91), channel_id=1, source_target_pairs={{0,16},{16,32},{32,48},{48,64},{64,80},{80,96},{96,112},{1,17},{17... | collective-permute-start | bytes 786440 | tf_op jit(solution)/shard_map/ppermute | solution.py:17
  553.2 9.6 collective-permute-start.8
  557.0 5.8 collective-permute-start.9
  558.3 4.6 collective-permute-start.10
  560.9 4.9 collective-permute-start.11
  621.2 12.0 %collective-permute-start.12 = (f32[256]{0:T(256)S(1)}, f32[256]{0:T(256)S(1)}, u32[]{:S(2)}, u32[]{:S(2)}) collective-permute-start(f32[256]{0:T(256)S(1)} %bitcast.481), channel_id=1, source_target_pairs={{0,16},{16,32},{32,48},{48,64},{64,80},{80,96},{96,112},{1,17},{17... | collective-permute-start | bytes 3080 | tf_op jit(solution)/shard_map/ppermute | solution.py:17
  627.6 5.8 collective-permute-start.13
  628.9 4.5 collective-permute-start.14
  630.8 4.9 collective-permute-start.15
  845.7 10.4 %collective-permute-start.16 = (f32[256]{0:T(256)S(1)}, f32[256]{0:T(256)S(1)}, u32[]{:S(2)}, u32[]{:S(2)}) collective-permute-start(f32[256]{0:T(256)S(1)} %bitcast.482), channel_id=1, source_target_pairs={{0,16},{16,32},{32,48},{48,64},{64,80},{80,96},{96,112},{1,17},{17... | collective-permute-start | bytes 3080 | tf_op jit(solution)/shard_map/ppermute | solution.py:17
  849.1 7.1 collective-permute-start.17
  850.4 5.8 collective-permute-start.18
  853.9 4.9 collective-permute-start.19
  914.2 12.0 %collective-permute-start.20 = (f32[256]{0:T(256)S(1)}, f32[256]{0:T(256)S(1)}, u32[]{:S(2)}, u32[]{:S(2)}) collective-permute-start(f32[256]{0:T(256)S(1)} %bitcast.483), channel_id=1, source_target_pairs={{0,16},{16,32},{32,48},{48,64},{64,80},{80,96},{96,112},{1,17},{17... | collective-permute-start | bytes 3080 | tf_op jit(solution)/shard_map/ppermute | solution.py:17
  920.5 5.8 collective-permute-start.21
  921.8 4.5 collective-permute-start.22
  923.8 4.9 collective-permute-start.23
  (40 other events, 1252.1 us)
